TPU v7x, 32 devices: a whole 2x2x4 slice. The times are simulated.
32 devices in a mesh: dp: 4 (over z), seq: 8 (over y, x, core).
Axes of the slice: x: 2, y: 2, z: 4, core: 2. Of those that a mesh axis runs over, the one named last changes fastest.
Arguments:
- tokens: float32 [4, 1024, 2048], P('dp', 'seq'), may hold values from -10 to 10, as said below
- cotangent: float32 [4, 1024, 2048], P('dp', 'seq'), may hold values from -6 to 6
- short_weights: float32 [3, 8, 2048], replicated, may hold values from 0.2 to 0.6
Outputs:
- grad_tokens: float32 [4, 1024, 2048], P('dp', 'seq')
- grad_weights: float32 [3, 8, 2048], P(None, None, 'seq')
Inputs may be any that keep to these rules, and one draw needn't show every extreme that they name: `tokens`: Real-valued activations of order one.
All inputs are finite; a program needn't handle non-finite values.
Results may differ from a plain program's by a relative error of at most 0.0003.
Values sent between devices are 32-bit elements; how exact they have to be, the bound alone decides.
No kernel may reach another device: no remote copies, remote signals or barrier semaphores. Data moves between devices by JAX's collectives and lax.ppermute only.
A program may use at most 64 MiB of HBM per device.

v0:
```python
import jax
import jax.numpy as jnp
from jax import lax
from jax.sharding import PartitionSpec as P

HEAD = 64
D = 2048
K = 8


def attend_back(query, key, value, grad_o):
    scale = HEAD ** (-0.5)
    hi = lax.Precision.HIGHEST
    scores = scale * jnp.einsum("qhe,khe->hqk", query, key, precision=hi)
    top = jnp.max(scores, axis=-1, keepdims=True)
    expo = jnp.exp(scores - top)
    probs = expo / jnp.sum(expo, axis=-1, keepdims=True)
    grad_probs = jnp.einsum("qhe,khe->hqk", grad_o, value, precision=hi)
    delta = jnp.sum(probs * grad_probs, axis=-1, keepdims=True)
    grad_scores = probs * (grad_probs - delta)
    grad_q = scale * jnp.einsum("hqk,khe->qhe", grad_scores, key, precision=hi)
    grad_k = scale * jnp.einsum("hqk,qhe->khe", grad_scores, query, precision=hi)
    grad_v = jnp.einsum("hqk,qhe->khe", probs, grad_o, precision=hi)
    return (grad_q, grad_k, grad_v)


def head_backward(query, key, value, grad_o):
    batch, sums, width = query.shape
    heads_here = width // HEAD

    def one_sequence(parts):
        shaped = [p.reshape(sums, heads_here, HEAD) for p in parts]
        grads = attend_back(shaped[0], shaped[1], shaped[2], shaped[3])
        return tuple((g.reshape(sums, width) for g in grads))

    return jax.vmap(one_sequence)((query, key, value, grad_o))


def per_device(tokens, cotangent, short_weights):
    hi = lax.Precision.HIGHEST
    batch = tokens.shape[0]
    col_tokens, col_grad = (
        lax.all_to_all(tokens, "seq", split_axis=2, concat_axis=1, tiled=True),
        lax.all_to_all(cotangent, "seq", split_axis=2, concat_axis=1, tiled=True),
    )
    length = col_tokens.shape[1]
    width = col_tokens.shape[2]
    sums = length // K
    start = lax.axis_index("seq") * width
    local_weights = lax.dynamic_slice_in_dim(short_weights, start, width, 2)
    grouped = col_tokens.reshape(batch, sums, K, width)
    summary = jnp.einsum("bjic,mic->mbjc", grouped, local_weights, precision=hi)
    grad_o = jnp.sum(col_grad.reshape(batch, sums, K, width), axis=2)
    grad_q, grad_k, grad_v = head_backward(summary[0], summary[1], summary[2], grad_o)
    grad_summary = jnp.stack([grad_q, grad_k, grad_v])
    grad_cols = jnp.einsum("mbjc,mic->bjic", grad_summary, local_weights, precision=hi).reshape(
        batch, length, width
    )
    grad_tokens = lax.all_to_all(grad_cols, "seq", split_axis=1, concat_axis=2, tiled=True)
    partial_value = jnp.einsum("mbjc,bjic->mic", grad_summary, grouped, precision=hi)
    raw = lax.psum(partial_value, "dp")
    total_sq = lax.psum(jnp.sum(raw * raw), "seq")
    mean_sq = total_sq / (3 * K * D)
    factor = jnp.minimum(1.0, 1.0 / jnp.sqrt(mean_sq + 1e-06))
    return (grad_tokens, raw * factor)


def solution(mesh):
    return jax.shard_map(
        per_device,
        mesh=mesh,
        in_specs=(P("dp", "seq", None), P("dp", "seq", None), P()),
        out_specs=(P("dp", "seq", None), P(None, None, "seq")),
        check_vma=False,
    )
```

profile of v0, /device:TPU:0, one launch (start us, length us, event | category | flops | bytes accessed | tf_op | source)
XLA Modules:
  0.0 110.5 jit_solution(7120607152902859944)
XLA Ops:
  0.6 3.6 %copy.65 = f32[1,128,2048]{1,0,2:T(1,128)} copy(f32[1,128,2048]{2,1,0:T(8,128)} %param.4) | data formatting | bytes 2097152 | tf_op args[1]
  4.3 5.3 %all-to-all-start.1 = ((f32[1,128,2048]{1,0,2:T(1,128)}), f32[1,128,2048]{1,0,2:T(1,128)S(1)}, u32[]{:S(2)}, u32[]{:S(2)}) async-start(f32[1,128,2048]{1,0,2:T(1,128)} %copy.65), calls=%async_computation.1 | async-start | bytes 2097152 | tf_op jit(solution)/shard_map/all_to_all | solution.py:44
  9.6 1.9 %copy.62 = f32[1,128,2048]{1,0,2:T(1,128)} copy(f32[1,128,2048]{2,1,0:T(8,128)S(1)} %copy-done.1) | data formatting | bytes 2097152 | tf_op args[0]
  11.5 13.5 %all-to-all-done.1 = f32[1,128,2048]{1,0,2:T(1,128)S(1)} async-done(((f32[1,128,2048]{1,0,2:T(1,128)}), f32[1,128,2048]{1,0,2:T(1,128)S(1)}, u32[]{:S(2)}, u32[]{:S(2)}) %all-to-all-start.1) | async-done | bytes 1048608 | tf_op jit(solution)/shard_map/all_to_all | solution.py:44
  25.0 3.6 %all-to-all-start = ((f32[1,128,2048]{1,0,2:T(1,128)}), f32[1,128,2048]{1,0,2:T(1,128)S(1)}, u32[]{:S(2)}, u32[]{:S(2)}) async-start(f32[1,128,2048]{1,0,2:T(1,128)} %copy.62), calls=%async_computation | async-start | bytes 2097152 | tf_op jit(solution)/shard_map/all_to_all | solution.py:43
  28.8 1.3 %copy.66 = f32[1,8,128,256]{3,2,1,0:T(8,128)} copy(f32[1,8,128,256]{2,3,1,0:T(8,128)S(1)} %bitcast.64) | data formatting | bytes 2097152 | tf_op jit(solution)/shard_map/all_to_all | solution.py:44
  30.1 1.5 %reduce_sum.37 = f32[128,256]{1,0:T(8,128)S(1)} reduce(f32[128,8,256]{2,1,0:T(8,128)} %bitcast.65, f32[]{:T(128)} %constant.6.clone.1), dimensions={1}, to_apply=%region_2.0 | reduce | flops 229376 | bytes 1179652 | tf_op jit(solution)/shard_map/reduce_sum | solution.py:53
  31.7 12.2 %all-to-all-done = f32[1,128,2048]{1,0,2:T(1,128)S(1)} async-done(((f32[1,128,2048]{1,0,2:T(1,128)}), f32[1,128,2048]{1,0,2:T(1,128)S(1)}, u32[]{:S(2)}, u32[]{:S(2)}) %all-to-all-start) | async-done | bytes 1048608 | tf_op jit(solution)/shard_map/all_to_all | solution.py:43
  44.2 0.6 copy.64
  44.8 1.8 %convolution_bitcast_fusion.2 = f32[3,1,128,256]{2,0,3,1:T(4,128)S(1)} fusion(f32[3,8,256]{1,0,2:T(4,128)S(1)} %copy.84, f32[128,8,256]{0,1,2:T(8,128)S(1)} %copy.64), kind=kOutput, calls=%fused_computation.2 | convolution fusion | flops 9437184 | bytes 1466368 | tf_op jit(solution)/shard_map/bjic,mic->mbjc/dot_general | solution.py:52
  46.8 0.6 fusion.9
  47.5 0.6 fusion.5
  48.1 0.6 multiply_reduce_fusion.1
  48.7 0.6 convolution_multiply_fusion.1
  50.4 3.4 %convolution_bitcast_fusion = f32[1,128,8,256]{1,2,3,0:T(8,128)} fusion(f32[3,8,256]{1,0,2:T(4,128)S(1)} %copy.84, f32[1,1,128,256]{2,0,3,1:T(1,128)S(1)} %bitcast.74, f32[1,1,128,256]{2,0,3,1:T(1,128)S(1)} %bitcast.76, f32[1,1,128,256]{2,0,3,1:T(1,128)S(1)} %bitcast.78), kind=kOutput, calls=%fused_computation | convolution fusion | flops 9633792 | bytes 1466368 | tf_op jit(solution)/shard_map/mbjc,mic->bjic/dot_general | solution.py:56
  53.8 1.7 %copy.74 = f32[1,128,8,256]{3,2,1,0:T(8,128)S(1)} copy(f32[1,128,8,256]{1,2,3,0:T(8,128)} %convolution_bitcast_fusion) | data formatting | bytes 2097152 | tf_op jit(solution)/shard_map/mbjc,mic->bjic/transpose | solution.py:56
  55.6 2.0 %copy.75 = f32[1,1024,256]{2,0,1:T(1,128)} copy(f32[1,1024,256]{2,1,0:T(8,128)S(1)} %bitcast.67) | data formatting | bytes 2097152 | tf_op jit(solution)/shard_map/reshape | solution.py:56
  57.6 3.9 %all-to-all-start.2 = ((f32[1,1024,256]{2,0,1:T(1,128)}), f32[1,1024,256]{2,0,1:T(1,128)S(1)}, u32[]{:S(2)}, u32[]{:S(2)}) async-start(f32[1,1024,256]{2,0,1:T(1,128)} %copy.75), calls=%async_computation.2 | async-start | bytes 2097152 | tf_op jit(solution)/shard_map/all_to_all | solution.py:59
  61.5 2.0 %convolution_bitcast_fusion.1 = f32[3,8,256]{1,0,2:T(4,128)S(1)} fusion(f32[128,8,256]{0,1,2:T(8,128)S(1)} %copy.64, f32[1,1,128,256]{2,0,3,1:T(1,128)S(1)} %bitcast.75, f32[1,1,128,256]{2,0,3,1:T(1,128)S(1)} %bitcast.77, f32[1,1,128,256]{2,0,3,1:T(1,128)S(1)} %bitcast.79), kind=kOutput, calls=%fused_computation.1 | convolution fusion | flops 9633792 | bytes 1466368 | tf_op jit(solution)/shard_map/mbjc,bjic->mic/dot_general | solution.py:60
  63.5 30.4 %psum.14 = f32[3,8,256]{1,0,2:T(4,128)S(1)} all-reduce(f32[3,8,256]{1,0,2:T(4,128)S(1)} %convolution_bitcast_fusion.1), channel_id=1, replica_groups=mesh['dp'=4,'seq'=8] {'dp'}, use_global_device_ids=true, to_apply=%region_4.0 | all-reduce | flops 6144 | bytes 49152 | tf_op jit(solution)/shard_map/psum | solution.py:61
  94.0 0.9 multiply_reduce_fusion
  94.8 12.4 %psum.15 = f32[]{:T(128)} all-reduce(f32[]{:T(128)} %multiply_reduce_fusion), channel_id=1, replica_groups=mesh['dp'=4,'seq'=8] {'seq'}, use_global_device_ids=true, to_apply=%region_6.0 | all-reduce | flops 1 | bytes 8 | tf_op jit(solution)/shard_map/psum | solution.py:62
  108.0 0.8 copy.79
  109.2 1.3 %copy.78 = f32[1,128,2048]{2,1,0:T(8,128)} copy(f32[1,128,2048]{1,2,0:T(8,128)S(1)} %bitcast.69) | data formatting | bytes 2097152
  (23 shorter events, 2.6 us)
Async XLA Ops:
  0.6 27.9 %copy-start = (f32[3,8,2048]{2,1,0:T(8,128)S(1)}, f32[3,8,2048]{2,1,0:T(8,128)}, u32[]{:S(2)}) copy-start(f32[3,8,2048]{2,1,0:T(8,128)} %param.5) | copy-start | bytes 589828
  4.3 5.3 %copy-start.1 = (f32[1,128,2048]{2,1,0:T(8,128)S(1)}, f32[1,128,2048]{2,1,0:T(8,128)}, u32[]{:S(2)}) copy-start(f32[1,128,2048]{2,1,0:T(8,128)} %param.3) | copy-start | bytes 3145732
  4.3 20.7 %all-to-all-start.1 = ((f32[1,128,2048]{1,0,2:T(1,128)}), f32[1,128,2048]{1,0,2:T(1,128)S(1)}, u32[]{:S(2)}, u32[]{:S(2)}) async-start(f32[1,128,2048]{1,0,2:T(1,128)} %copy.65), calls=%async_computation.1 | async-start | bytes 2097152 | tf_op jit(solution)/shard_map/all_to_all | solution.py:44
  25.0 18.9 %all-to-all-start = ((f32[1,128,2048]{1,0,2:T(1,128)}), f32[1,128,2048]{1,0,2:T(1,128)S(1)}, u32[]{:S(2)}, u32[]{:S(2)}) async-start(f32[1,128,2048]{1,0,2:T(1,128)} %copy.62), calls=%async_computation | async-start | bytes 2097152 | tf_op jit(solution)/shard_map/all_to_all | solution.py:43
  49.4 0.6 copy-start.2
  49.8 0.7 copy-start.4
  57.6 3.9 %copy-start.3 = (f32[4,64,128]{2,1,0:T(8,128)S(1)}, f32[4,64,128]{2,1,0:T(8,128)}, u32[]{:S(2)}) copy-start(f32[4,64,128]{2,1,0:T(8,128)} %copy-done.2) | copy-start | bytes 393220
  57.6 3.9 %copy-start.5 = (f32[4,64,128]{2,1,0:T(8,128)S(1)}, f32[4,64,128]{2,1,0:T(8,128)}, u32[]{:S(2)}) copy-start(f32[4,64,128]{2,1,0:T(8,128)} %copy-done.4) | copy-start | bytes 393220
  57.6 51.2 %all-to-all-start.2 = ((f32[1,1024,256]{2,0,1:T(1,128)}), f32[1,1024,256]{2,0,1:T(1,128)S(1)}, u32[]{:S(2)}, u32[]{:S(2)}) async-start(f32[1,1024,256]{2,0,1:T(1,128)} %copy.75), calls=%async_computation.2 | async-start | bytes 2097152 | tf_op jit(solution)/shard_map/all_to_all | solution.py:59
where the time goes:
time: 111 us
  blocking collectives  42.8 us (39%)
  waiting for transfers between devices  25.6 us (23%)
  local copies, waits for them, and re-layouts  15.2 us (14%)
  starting transfers between devices  12.8 us (12%)
  matrix products  10 us (9%)
  other arithmetic  2.51 us (2%)
  between operations  1.53 us (1%)
    psum x1, blocking collectives, per_device(): raw = lax.psum(partial_value, 'dp')  30.4 us
    all_to_all x1, waiting for transfers between devices, per_device(): lax.all_to_all(cotangent, 'seq', split_axis=2, concat_axis=1, tiled=True)  13.5 us
    psum x1, blocking collectives, per_device(): total_sq = lax.psum(jnp.sum(raw * raw), 'seq')  12.4 us
    all_to_all x1, waiting for transfers between devices, per_device(): lax.all_to_all(tokens, 'seq', split_axis=2, concat_axis=1, tiled=True)  12.2 us
    unnamed x18, local copies, waits for them, and re-layouts  8.56 us
    all_to_all x1, starting transfers between devices, per_device(): lax.all_to_all(cotangent, 'seq', split_axis=2, concat_axis=1, tiled=True)  5.33 us
    all_to_all x1, starting transfers between devices, per_device(): lax.all_to_all(grad_cols, 'seq', split_axis=1, concat_axis=2, tiled=True)  3.87 us
    all_to_all x1, starting transfers between devices, per_device(): lax.all_to_all(tokens, 'seq', split_axis=2, concat_axis=1, tiled=True)  3.56 us
  transfers between devices with their start and end apart: 3, of which 2 were waited for; matrix products, arithmetic and copies ran while one was open for 8% of the time, Pallas kernels for 0%

commit v1 on v0

--- a/solution.py
+++ b/solution.py
@@ -6,6 +6,14 @@
 HEAD = 64
 D = 2048
 K = 8
+
+
+def sum_by_hops(x, mesh_axis):
+    devices, acc = (lax.axis_size(mesh_axis), x)
+    for reach in [1 << k for k in range(devices.bit_length() - 1)]:
+        swap = [(i, i ^ reach) for i in range(devices)]
+        acc = acc + lax.ppermute(acc, mesh_axis, swap)
+    return acc
 
 
 def attend_back(query, key, value, grad_o):
@@ -58,7 +66,7 @@
     )
     grad_tokens = lax.all_to_all(grad_cols, "seq", split_axis=1, concat_axis=2, tiled=True)
     partial_value = jnp.einsum("mbjc,bjic->mic", grad_summary, grouped, precision=hi)
-    raw = lax.psum(partial_value, "dp")
+    raw = sum_by_hops(partial_value, "dp")
     total_sq = lax.psum(jnp.sum(raw * raw), "seq")
     mean_sq = total_sq / (3 * K * D)
     factor = jnp.minimum(1.0, 1.0 / jnp.sqrt(mean_sq + 1e-06))

time: 111 us -> 120 us (1.081)
  waiting for transfers between devices: 25.6 us -> 60.9 us
  blocking collectives: 42.8 us -> 13.5 us
  starting transfers between devices: 12.8 us -> 16.9 us
    ppermute x0 -> x2, waiting for transfers between devices: none -> 35.2 us  [sum_by_hops(): acc = acc + lax.ppermute(acc, mesh_axis, swap)]
    psum x1 -> x0, blocking collectives: 30.4 us -> none  [per_device(): raw = lax.psum(partial_value, 'dp')]
    ppermute x0 -> x2, starting transfers between devices: none -> 4.29 us  [sum_by_hops(): acc = acc + lax.ppermute(acc, mesh_axis, swap)]
    unnamed x18 -> x10, local copies, waits for them, and re-layouts: 8.56 us -> 7.91 us
  transfers between devices with their start and end apart: 3 -> 5, of which waited for: 2 -> 4; matrix products, arithmetic and copies ran while one was open for 8% -> 7% of each run, Pallas kernels for 0% -> 0%
where the time goes in v1:
time: 120 us
  waiting for transfers between devices  60.9 us (51%)
  starting transfers between devices  16.9 us (14%)
  local copies, waits for them, and re-layouts  14.6 us (12%)
  blocking collectives  13.5 us (11%)
  matrix products  10 us (8%)
  other arithmetic  2.65 us (2%)
  between operations  1.49 us (1%)
    ppermute x2, waiting for transfers between devices, sum_by_hops(): acc = acc + lax.ppermute(acc, mesh_axis, swap)  35.2 us
    psum x1, blocking collectives, per_device(): total_sq = lax.psum(jnp.sum(raw * raw), 'seq')  13.5 us
    all_to_all x1, waiting for transfers between devices, per_device(): lax.all_to_all(cotangent, 'seq', split_axis=2, concat_axis=1, tiled=True)  13.5 us
    all_to_all x1, waiting for transfers between devices, per_device(): lax.all_to_all(tokens, 'seq', split_axis=2, concat_axis=1, tiled=True)  12.2 us
    unnamed x10, local copies, waits for them, and re-layouts  7.91 us
    all_to_all x1, starting transfers between devices, per_device(): lax.all_to_all(cotangent, 'seq', split_axis=2, concat_axis=1, tiled=True)  5.33 us
    ppermute x2, starting transfers between devices, sum_by_hops(): acc = acc + lax.ppermute(acc, mesh_axis, swap)  4.29 us
    all_to_all x1, starting transfers between devices, per_device(): lax.all_to_all(grad_cols, 'seq', split_axis=1, concat_axis=2, tiled=True)  3.74 us
  transfers between devices with their start and end apart: 5, of which 4 were waited for; matrix products, arithmetic and copies ran while one was open for 7% of the time, Pallas kernels for 0%

profile of v1, /device:TPU:0, one launch (start us, length us, event | category | flops | bytes accessed | tf_op | source)
XLA Modules:
  0.0 120.0 jit_solution(6242271097735200544)
XLA Ops:
  0.6 3.6 %copy.65 = f32[1,128,2048]{1,0,2:T(1,128)} copy(f32[1,128,2048]{2,1,0:T(8,128)} %param.4) | data formatting | bytes 2097152 | tf_op args[1]
  4.3 5.3 %all-to-all-start.1 = ((f32[1,128,2048]{1,0,2:T(1,128)}), f32[1,128,2048]{1,0,2:T(1,128)S(1)}, u32[]{:S(2)}, u32[]{:S(2)}) async-start(f32[1,128,2048]{1,0,2:T(1,128)} %copy.65), calls=%async_computation.1 | async-start | bytes 2097152 | tf_op jit(solution)/shard_map/all_to_all | solution.py:52
  9.6 1.9 %copy.62 = f32[1,128,2048]{1,0,2:T(1,128)} copy(f32[1,128,2048]{2,1,0:T(8,128)S(1)} %copy-done.1) | data formatting | bytes 2097152 | tf_op args[0]
  11.5 13.5 %all-to-all-done.1 = f32[1,128,2048]{1,0,2:T(1,128)S(1)} async-done(((f32[1,128,2048]{1,0,2:T(1,128)}), f32[1,128,2048]{1,0,2:T(1,128)S(1)}, u32[]{:S(2)}, u32[]{:S(2)}) %all-to-all-start.1) | async-done | bytes 1048608 | tf_op jit(solution)/shard_map/all_to_all | solution.py:52
  25.0 3.6 %all-to-all-start = ((f32[1,128,2048]{1,0,2:T(1,128)}), f32[1,128,2048]{1,0,2:T(1,128)S(1)}, u32[]{:S(2)}, u32[]{:S(2)}) async-start(f32[1,128,2048]{1,0,2:T(1,128)} %copy.62), calls=%async_computation | async-start | bytes 2097152 | tf_op jit(solution)/shard_map/all_to_all | solution.py:51
  28.8 1.3 %copy.66 = f32[1,8,128,256]{3,2,1,0:T(8,128)} copy(f32[1,8,128,256]{2,3,1,0:T(8,128)S(1)} %bitcast.64) | data formatting | bytes 2097152 | tf_op jit(solution)/shard_map/all_to_all | solution.py:52
  30.1 1.5 %reduce_sum.37 = f32[128,256]{1,0:T(8,128)S(1)} reduce(f32[128,8,256]{2,1,0:T(8,128)} %bitcast.65, f32[]{:T(128)} %constant.6.clone.1), dimensions={1}, to_apply=%region_2.0 | reduce | flops 229376 | bytes 1179652 | tf_op jit(solution)/shard_map/reduce_sum | solution.py:61
  31.7 12.2 %all-to-all-done = f32[1,128,2048]{1,0,2:T(1,128)S(1)} async-done(((f32[1,128,2048]{1,0,2:T(1,128)}), f32[1,128,2048]{1,0,2:T(1,128)S(1)}, u32[]{:S(2)}, u32[]{:S(2)}) %all-to-all-start) | async-done | bytes 1048608 | tf_op jit(solution)/shard_map/all_to_all | solution.py:51
  44.8 1.8 %convolution_bitcast_fusion.2 = f32[3,1,128,256]{2,0,3,1:T(4,128)S(1)} fusion(f32[3,8,256]{1,0,2:T(4,128)S(1)} %copy.84, f32[128,8,256]{0,1,2:T(8,128)S(1)} %copy.64), kind=kOutput, calls=%fused_computation.2 | convolution fusion | flops 9437184 | bytes 1466368 | tf_op jit(solution)/shard_map/bjic,mic->mbjc/dot_general | solution.py:60
  48.1 0.6 multiply_reduce_fusion.1
  48.7 0.6 convolution_multiply_fusion.1
  49.8 3.4 %convolution_bitcast_fusion = f32[1,128,8,256]{1,2,3,0:T(8,128)} fusion(f32[3,8,256]{1,0,2:T(4,128)S(1)} %copy.84, f32[1,1,128,256]{2,0,3,1:T(1,128)S(1)} %bitcast.74, f32[1,1,128,256]{2,0,3,1:T(1,128)S(1)} %bitcast.76, f32[1,1,128,256]{2,0,3,1:T(1,128)S(1)} %bitcast.78), kind=kOutput, calls=%fused_computation | convolution fusion | flops 9633792 | bytes 1466368 | tf_op jit(solution)/shard_map/mbjc,mic->bjic/dot_general | solution.py:64
  53.2 1.7 %copy.74 = f32[1,128,8,256]{3,2,1,0:T(8,128)S(1)} copy(f32[1,128,8,256]{1,2,3,0:T(8,128)} %convolution_bitcast_fusion) | data formatting | bytes 2097152 | tf_op jit(solution)/shard_map/mbjc,mic->bjic/transpose | solution.py:64
  54.9 2.0 %copy.75 = f32[1,1024,256]{2,0,1:T(1,128)} copy(f32[1,1024,256]{2,1,0:T(8,128)S(1)} %bitcast.67) | data formatting | bytes 2097152 | tf_op jit(solution)/shard_map/reshape | solution.py:64
  57.0 3.7 %all-to-all-start.2 = ((f32[1,1024,256]{2,0,1:T(1,128)}), f32[1,1024,256]{2,0,1:T(1,128)S(1)}, u32[]{:S(2)}, u32[]{:S(2)}) async-start(f32[1,1024,256]{2,0,1:T(1,128)} %copy.75), calls=%async_computation.2 | async-start | bytes 2097152 | tf_op jit(solution)/shard_map/all_to_all | solution.py:67
  60.7 2.0 %convolution_bitcast_fusion.1 = f32[3,8,256]{1,0,2:T(4,128)S(1)} fusion(f32[128,8,256]{0,1,2:T(8,128)S(1)} %copy.64, f32[1,1,128,256]{2,0,3,1:T(1,128)S(1)} %bitcast.75, f32[1,1,128,256]{2,0,3,1:T(1,128)S(1)} %bitcast.77, f32[1,1,128,256]{2,0,3,1:T(1,128)S(1)} %bitcast.79), kind=kOutput, calls=%fused_computation.1 | convolution fusion | flops 9633792 | bytes 1466368 | tf_op jit(solution)/shard_map/mbjc,bjic->mic/dot_general | solution.py:68
  62.7 1.6 %collective-permute-start = (f32[3,8,256]{1,0,2:T(4,128)S(1)}, f32[3,8,256]{1,0,2:T(4,128)S(1)}, u32[]{:S(2)}, u32[]{:S(2)}) collective-permute-start(f32[3,8,256]{1,0,2:T(4,128)S(1)} %convolution_bitcast_fusion.1), channel_id=1, source_target_pairs={{0,8},{8,0},{16,24},{24,16},{1,9},{9,1},{17,25},{25,17},{2,10},{10... | collective-permute-start | bytes 73736 | tf_op jit(solution)/shard_map/ppermute | solution.py:15
  64.4 12.5 %collective-permute-done = f32[3,8,256]{1,0,2:T(4,128)S(1)} collective-permute-done((f32[3,8,256]{1,0,2:T(4,128)S(1)}, f32[3,8,256]{1,0,2:T(4,128)S(1)}, u32[]{:S(2)}, u32[]{:S(2)}) %collective-permute-start) | collective-permute-done | bytes 24608 | tf_op jit(solution)/shard_map/ppermute | solution.py:15
  77.0 2.7 %collective-permute-start.1 = (f32[3,8,256]{1,0,2:T(4,128)S(1)}, f32[3,8,256]{1,0,2:T(4,128)S(1)}, u32[]{:S(2)}, u32[]{:S(2)}) collective-permute-start(f32[3,8,256]{1,0,2:T(4,128)S(1)} %add.15), channel_id=1, source_target_pairs={{0,16},{8,24},{16,0},{24,8},{1,17},{9,25},{17,1},{25,9},{2,18},{10... | collective-permute-start | bytes 73736 | tf_op jit(solution)/shard_map/ppermute | solution.py:15
  79.7 22.7 %collective-permute-done.1 = f32[3,8,256]{1,0,2:T(4,128)S(1)} collective-permute-done((f32[3,8,256]{1,0,2:T(4,128)S(1)}, f32[3,8,256]{1,0,2:T(4,128)S(1)}, u32[]{:S(2)}, u32[]{:S(2)}) %collective-permute-start.1) | collective-permute-done | bytes 24608 | tf_op jit(solution)/shard_map/ppermute | solution.py:15
  102.4 0.9 multiply_reduce_fusion
  103.3 13.5 %psum.7 = f32[]{:T(128)} all-reduce(f32[]{:T(128)} %get-tuple-element.12), channel_id=1, replica_groups=mesh['dp'=4,'seq'=8] {'seq'}, use_global_device_ids=true, to_apply=%region_5.0 | all-reduce | flops 1 | bytes 8 | tf_op jit(solution)/shard_map/psum | solution.py:70
  117.5 0.8 copy.79
  118.7 1.3 %copy.78 = f32[1,128,2048]{2,1,0:T(8,128)} copy(f32[1,128,2048]{1,2,0:T(8,128)S(1)} %bitcast.69) | data formatting | bytes 2097152
  (19 shorter events, 3.8 us)
Async XLA Ops:
  0.6 27.9 %copy-start = (f32[3,8,2048]{2,1,0:T(8,128)S(1)}, f32[3,8,2048]{2,1,0:T(8,128)}, u32[]{:S(2)}) copy-start(f32[3,8,2048]{2,1,0:T(8,128)} %param.5) | copy-start | bytes 589828
  4.3 5.3 %copy-start.1 = (f32[1,128,2048]{2,1,0:T(8,128)S(1)}, f32[1,128,2048]{2,1,0:T(8,128)}, u32[]{:S(2)}) copy-start(f32[1,128,2048]{2,1,0:T(8,128)} %param.3) | copy-start | bytes 3145732
  4.3 20.7 %all-to-all-start.1 = ((f32[1,128,2048]{1,0,2:T(1,128)}), f32[1,128,2048]{1,0,2:T(1,128)S(1)}, u32[]{:S(2)}, u32[]{:S(2)}) async-start(f32[1,128,2048]{1,0,2:T(1,128)} %copy.65), calls=%async_computation.1 | async-start | bytes 2097152 | tf_op jit(solution)/shard_map/all_to_all | solution.py:52
  25.0 18.9 %all-to-all-start = ((f32[1,128,2048]{1,0,2:T(1,128)}), f32[1,128,2048]{1,0,2:T(1,128)S(1)}, u32[]{:S(2)}, u32[]{:S(2)}) async-start(f32[1,128,2048]{1,0,2:T(1,128)} %copy.62), calls=%async_computation | async-start | bytes 2097152 | tf_op jit(solution)/shard_map/all_to_all | solution.py:51
  57.0 61.3 %all-to-all-start.2 = ((f32[1,1024,256]{2,0,1:T(1,128)}), f32[1,1024,256]{2,0,1:T(1,128)S(1)}, u32[]{:S(2)}, u32[]{:S(2)}) async-start(f32[1,1024,256]{2,0,1:T(1,128)} %copy.75), calls=%async_computation.2 | async-start | bytes 2097152 | tf_op jit(solution)/shard_map/all_to_all | solution.py:67
  62.7 14.1 %collective-permute-start = (f32[3,8,256]{1,0,2:T(4,128)S(1)}, f32[3,8,256]{1,0,2:T(4,128)S(1)}, u32[]{:S(2)}, u32[]{:S(2)}) collective-permute-start(f32[3,8,256]{1,0,2:T(4,128)S(1)} %convolution_bitcast_fusion.1), channel_id=1, source_target_pairs={{0,8},{8,0},{16,24},{24,16},{1,9},{9,1},{17,25},{25,17},{2,10},{10... | collective-permute-start | bytes 73736 | tf_op jit(solution)/shard_map/ppermute | solution.py:15
  77.0 25.4 %collective-permute-start.1 = (f32[3,8,256]{1,0,2:T(4,128)S(1)}, f32[3,8,256]{1,0,2:T(4,128)S(1)}, u32[]{:S(2)}, u32[]{:S(2)}) collective-permute-start(f32[3,8,256]{1,0,2:T(4,128)S(1)} %add.15), channel_id=1, source_target_pairs={{0,16},{8,24},{16,0},{24,8},{1,17},{9,25},{17,1},{25,9},{2,18},{10... | collective-permute-start | bytes 73736 | tf_op jit(solution)/shard_map/ppermute | solution.py:15
